TPU v7x, 1024 devices: a whole 4x4x32 slice. The times are simulated.
1024 devices in a mesh: dp: 2 (over z_hi), dom: 64 (over z_lo, y), tensor: 8 (over x, core).
Axes of the slice: x: 4, y: 4, z: 32 (z_hi: 2, z_lo: 16; z = z_hi * 16 + z_lo), core: 2. Of those that a mesh axis runs over, the one named last changes fastest.
Arguments:
- states: bfloat16 [2, 32768, 512], P('dp', 'dom'), may hold values from -60 to 60, as said below
- w_query: bfloat16 [512, 512], P(None, 'tensor'), as said below
- w_key: bfloat16 [512, 512], P(None, 'tensor'), as said below
- w_value: bfloat16 [512, 512], P(None, 'tensor'), may hold values from -0.25 to 0.25
- w_out: bfloat16 [512, 512], P('tensor'), may hold values from -0.25 to 0.25
- send_blocks: int32 [64, 4, 2], P('dom'), may hold values from 0 to 3
- neighbor_blocks: int32 [256, 3], P('dom'), may hold values from 0 to 11, as said below
- cotangent: bfloat16 [2, 32768, 512], P('dp', 'dom'), may hold values from -6 to 6
Outputs:
- update: bfloat16 [2, 32768, 512], P('dp', 'dom', 'tensor')
- branch_grad: bfloat16 [2, 32768, 512], P('dp', 'dom', 'tensor')
- grad_query: float32 [512, 512], P(None, 'tensor')
- grad_key: float32 [512, 512], P(None, 'tensor')
- grad_value: float32 [512, 512], P(None, 'tensor')
- grad_out: float32 [512, 512], P('tensor')
Inputs may be any that keep to these rules, and one draw needn't show every extreme that they name: `neighbor_blocks`: entries index the pool of the row's own partition; every pool entry from 4 on is named by some row of that partition. `states`: real entries. `w_query`: real entries. `w_key`: real entries.
All inputs are finite; a program needn't handle non-finite values.
Results may differ from a plain program's by a relative error of at most 0.02.
The roundings to bfloat16 on the way count: a program that leaves them out, or rounds other values in their place, can miss the bound.
Values may be sent and summed in bfloat16 or wider, within the bound.
A program may use at most 32 MiB of HBM per device.

v0:
```python
import math

import jax
import jax.numpy as jnp
from jax import lax
from jax.sharding import PartitionSpec as P

BLK = 128
HOPS = 2
SEND = 2
HD = 64


def shifted(block, axis, distance):
    devices = range(lax.axis_size(axis))
    route = [((i - distance) % len(devices), i) for i in devices]
    return lax.ppermute(block, axis, route)


def offset_list(hops):
    result = []
    for section in range(1, hops + 1):
        result.append(section)
        result.append(-section)
    return result


def normalize(states):
    values = states.astype(jnp.float32)
    inverse = lax.rsqrt(jnp.mean(values * values, axis=-1, keepdims=True) + 1e-05)
    return (values * inverse, inverse)


def product(form, left, right):
    return jnp.einsum(form, left, right, preferred_element_type=jnp.float32)


def attend(queries, key_pool, key_index, grad_heads, head_count):
    replicas, blocks, block_rows, widths = queries.shape
    head_size = widths // head_count
    shrink = 1.0 / math.sqrt(head_size)
    listed = key_index.shape[1]
    chosen = jnp.take(key_pool, key_index.reshape(-1), axis=1)
    chosen = chosen.reshape(replicas, blocks, listed * block_rows, 2, head_count, head_size)
    key_rows = chosen[:, :, :, 0]
    value_rows = chosen[:, :, :, 1]
    query_heads = queries.reshape(replicas, blocks, block_rows, head_count, head_size)
    grad_split = grad_heads.reshape(replicas, blocks, block_rows, head_count, head_size)
    scores = product("rbqhe,rbkhe->rbhqk", query_heads, key_rows) * shrink
    highest = jnp.max(scores, axis=-1, keepdims=True)
    powers = jnp.exp(scores - highest)
    weights = powers / jnp.sum(powers, axis=-1, keepdims=True)
    weights_low = weights.astype(jnp.bfloat16)
    mixed_rows = product("rbhqk,rbkhe->rbqhe", weights_low, value_rows).astype(jnp.bfloat16)
    prob_grad = product("rbqhe,rbkhe->rbhqk", grad_split, value_rows)
    score_grad = weights * (prob_grad - jnp.sum(weights * prob_grad, axis=-1, keepdims=True))
    score_low = (score_grad * shrink).astype(jnp.bfloat16)
    query_grad = product("rbhqk,rbkhe->rbqhe", score_low, key_rows).astype(jnp.bfloat16)
    key_grad = product("rbhqk,rbqhe->rbkhe", score_low, query_heads)
    value_grad = product("rbhqk,rbqhe->rbkhe", weights_low, grad_split)
    chosen_grad = jnp.stack([key_grad, value_grad], axis=3).reshape(
        replicas, blocks, listed, block_rows, 2 * widths
    )
    pool_size = key_pool.shape[1]
    chooser = (
        key_index[:, :, None] == jnp.arange(pool_size, dtype=jnp.int32)[None, None, :]
    ).astype(jnp.float32)
    pool_grad = jnp.einsum("bnp,rbnqc->rpqc", chooser, chosen_grad, precision=lax.Precision.HIGHEST)
    return (
        mixed_rows.reshape(replicas, blocks, block_rows, widths),
        query_grad.reshape(replicas, blocks, block_rows, widths),
        pool_grad,
    )


def body(states, w_query, w_key, w_value, w_out, send_blocks, neighbor_blocks, cotangent):
    replicas, node_count, widths = states.shape
    local_width = w_query.shape[1]
    head_count = local_width // HD
    blocks = node_count // BLK
    normed, inverse = normalize(states)
    unit_rows = normed.astype(jnp.bfloat16)
    flat_unit = unit_rows.reshape(-1, widths)
    queries = jnp.dot(flat_unit, w_query, preferred_element_type=jnp.float32).astype(jnp.bfloat16)
    queries = queries.reshape(replicas, blocks, BLK, local_width)
    paired = jnp.dot(
        flat_unit, jnp.concatenate([w_key, w_value], axis=1), preferred_element_type=jnp.float32
    ).astype(jnp.bfloat16)
    paired = paired.reshape(replicas, blocks, BLK, 2 * local_width)
    flat_cot = cotangent.reshape(-1, widths)
    grad_heads = jnp.dot(flat_cot, w_out.T, preferred_element_type=jnp.float32).astype(jnp.bfloat16)
    grad_heads = grad_heads.reshape(replicas, blocks, BLK, local_width)
    offsets = offset_list(HOPS)
    outgoing = [
        jnp.take(paired, send_blocks[0, slot_group], axis=1) for slot_group in range(len(offsets))
    ]
    arrived = [None] * len(offsets)
    for slot_group in range(len(offsets)):
        arrived[slot_group] = shifted(outgoing[slot_group], "dom", offsets[slot_group])
    key_pool = jnp.concatenate([paired] + arrived, axis=1)
    own_blocks = jnp.arange(blocks, dtype=jnp.int32)[:, None]
    key_index = jnp.concatenate([own_blocks, neighbor_blocks], axis=1)
    mixed_rows, query_grad, pool_grad = attend(queries, key_pool, key_index, grad_heads, head_count)
    own_grad = pool_grad[:, :blocks]
    remote = pool_grad[:, blocks:].astype(jnp.bfloat16)
    leaving = [
        remote[:, slot_group * SEND : (slot_group + 1) * SEND] for slot_group in range(len(offsets))
    ]
    returned = [None] * len(offsets)
    for slot_group in range(len(offsets)):
        returned[slot_group] = shifted(leaving[slot_group], "dom", -offsets[slot_group])
    returned_stack = jnp.stack(returned, axis=1).astype(jnp.float32)
    chooser = (
        send_blocks[0][:, :, None] == jnp.arange(blocks, dtype=jnp.int32)[None, None, :]
    ).astype(jnp.float32)
    incoming = jnp.einsum(
        "icj,ricqe->rjqe", chooser, returned_stack, precision=lax.Precision.HIGHEST
    )
    pair_grad = (own_grad + incoming).astype(jnp.bfloat16).reshape(-1, 2 * local_width)
    key_grad = pair_grad[:, :local_width]
    value_grad = pair_grad[:, local_width:]
    flat_query_grad = query_grad.reshape(-1, local_width)
    flat_mixed = mixed_rows.reshape(-1, local_width)
    update_term = jnp.dot(flat_mixed, w_out, preferred_element_type=jnp.float32)
    unit_term = jnp.dot(flat_query_grad, w_query.T, preferred_element_type=jnp.float32)
    unit_term = unit_term + jnp.dot(key_grad, w_key.T, preferred_element_type=jnp.float32)
    unit_term = unit_term + jnp.dot(value_grad, w_value.T, preferred_element_type=jnp.float32)
    slab_width = widths // lax.axis_size("tensor")
    offset_start = lax.axis_index("tensor") * slab_width
    flat_normed = normed.reshape(-1, widths)
    normed_own = lax.dynamic_slice_in_dim(flat_normed, offset_start, slab_width, 1)
    update_sum, unit_sum = (
        lax.psum(update_term.astype(jnp.bfloat16), "tensor").astype(jnp.float32),
        lax.psum(unit_term.astype(jnp.bfloat16), "tensor").astype(jnp.float32),
    )
    row_mean = jnp.mean(unit_sum * flat_normed, axis=-1, keepdims=True)
    update_own = lax.dynamic_slice_in_dim(update_sum, offset_start, slab_width, 1)
    unit_own = lax.dynamic_slice_in_dim(unit_sum, offset_start, slab_width, 1)
    update = update_own.astype(jnp.bfloat16).reshape(replicas, node_count, slab_width)
    branch_grad = (inverse.reshape(-1, 1) * (unit_own - normed_own * row_mean)).astype(jnp.bfloat16)
    branch_grad = branch_grad.reshape(replicas, node_count, slab_width)
    total_rows = replicas * node_count * lax.axis_size("dp") * lax.axis_size("dom")
    factor = 1.0 / math.sqrt(total_rows)
    grad_terms = (
        jnp.dot(flat_unit.T, flat_query_grad, preferred_element_type=jnp.float32),
        jnp.dot(flat_unit.T, key_grad, preferred_element_type=jnp.float32),
        jnp.dot(flat_unit.T, value_grad, preferred_element_type=jnp.float32),
        jnp.dot(flat_mixed.T, flat_cot, preferred_element_type=jnp.float32),
    )
    summed_grads = lax.psum(
        (grad_terms[0], grad_terms[1], grad_terms[2], grad_terms[3]), ("dp", "dom")
    )
    return (
        update,
        branch_grad,
        summed_grads[0] * factor,
        summed_grads[1] * factor,
        summed_grads[2] * factor,
        summed_grads[3] * factor,
    )


def solution(mesh):
    placed = (
        P("dp", "dom", None),
        P(None, "tensor"),
        P(None, "tensor"),
        P(None, "tensor"),
        P("tensor", None),
        P("dom", None, None),
        P("dom", None),
        P("dp", "dom", None),
    )
    return jax.shard_map(
        body,
        mesh=mesh,
        in_specs=placed,
        out_specs=(
            P("dp", "dom", "tensor"),
            P("dp", "dom", "tensor"),
            P(None, "tensor"),
            P(None, "tensor"),
            P(None, "tensor"),
            P("tensor", None),
        ),
        check_vma=False,
    )
```

profile of v0, /device:TPU:6, one launch (start us, length us, event | category | flops | bytes accessed | tf_op | source)
XLA Modules:
  0.0 764.9 jit_solution(2055804028641647010)
XLA Ops:
  7.2 1.0 slice_reduce_fusion
  8.3 1.2 fusion.15
  9.6 1.2 convolution_convert_fusion.1
  10.8 0.6 gather_fusion.1
  11.4 3.5 collective-permute-start
  14.9 0.6 gather_fusion.2
  15.6 27.3 %collective-permute-start.1 = (bf16[1,2,128,128]{3,2,1,0:T(8,128)(2,1)S(1)}, bf16[1,2,128,128]{3,2,1,0:T(8,128)(2,1)S(1)}, u32[]{:S(2)}, u32[]{:S(2)}) collective-permute-start(bf16[1,2,128,128]{3,2,1,0:T(8,128)(2,1)S(1)} %bitcast_select_fusion.2), channel_id=1, source_target_pairs={{8,0},{16,8},{24,16},{32,24},{40,32},{48,40},{56,48},{64,56},{72,6... | collective-permute-start | bytes 196616 | tf_op jit(solution)/shard_map/ppermute | solution.py:17
  42.9 0.6 gather_fusion.3
  43.6 1.9 collective-permute-start.2
  45.5 0.6 gather_fusion.4
  46.2 22.7 %collective-permute-start.3 = (bf16[1,2,128,128]{3,2,1,0:T(8,128)(2,1)S(1)}, bf16[1,2,128,128]{3,2,1,0:T(8,128)(2,1)S(1)}, u32[]{:S(2)}, u32[]{:S(2)}) collective-permute-start(bf16[1,2,128,128]{3,2,1,0:T(8,128)(2,1)S(1)} %bitcast_select_fusion), channel_id=1, source_target_pairs={{16,0},{24,8},{32,16},{40,24},{48,32},{56,40},{64,48},{72,56},{80,... | collective-permute-start | bytes 196616 | tf_op jit(solution)/shard_map/ppermute | solution.py:17
  69.0 0.6 copy-done.11
  69.8 0.4 fusion.13
  70.2 0.8 copy-done.3
  71.4 0.6 gather_fusion
  72.1 0.4 reshape.290
  72.5 0.7 copy.33
  73.3 0.3 fusion.46
  73.7 1.5 fusion.100
  75.1 4.0 fusion.12
  79.2 4.2 convolution_bitcast_fusion.2
  83.3 1.7 fusion.11
  85.4 1.0 fusion.29
  86.9 1.3 reshape.210
  88.2 1.6 copy.41
  89.9 0.8 fusion.103
  91.0 3.6 collective-permute-start.4
  94.6 1.9 collective-permute-start.7
  96.5 22.5 %collective-permute-start.6 = (bf16[1,2,128,128]{3,1,2,0:T(2,128)(2,1)S(1)}, bf16[1,2,128,128]{3,1,2,0:T(2,128)(2,1)S(1)}, u32[]{:S(2)}, u32[]{:S(2)}) collective-permute-start(bf16[1,2,128,128]{3,1,2,0:T(2,128)(2,1)S(1)} %get-tuple-element.39), channel_id=1, source_target_pairs={{16,0},{24,8},{32,16},{40,24},{48,32},{56,40},{64,48},{72,56},{80,... | collective-permute-start | bytes 196616 | tf_op jit(solution)/shard_map/ppermute | solution.py:17
  119.0 2.3 collective-permute-start.5
  121.3 1.2 convolution_convert_fusion
  122.5 21.1 %collective-permute-done.5 = bf16[1,2,128,128]{3,1,2,0:T(2,128)(2,1)S(1)} collective-permute-done((bf16[1,2,128,128]{3,1,2,0:T(2,128)(2,1)S(1)}, bf16[1,2,128,128]{3,1,2,0:T(2,128)(2,1)S(1)}, u32[]{:S(2)}, u32[]{:S(2)}) %collective-permute-start.5) | collective-permute-done | bytes 65568 | tf_op jit(solution)/shard_map/ppermute | solution.py:17
  143.5 0.5 fusion.10
  144.1 0.8 copy-done.9
  145.1 0.6 copy-done.7
  145.7 1.1 fusion.7
  146.9 0.9 fusion.22
  147.8 1.0 fusion.27
  148.8 1.1 fusion.25
  150.0 92.7 %all-reduce.7.cloned.1.call-done = (bf16[512,512]{0,1:T(8,128)(2,1)}, bf16[512,512]{1,0:T(8,128)(2,1)}) async-done(((bf16[512,512]{0,1:T(8,128)(2,1)}, bf16[512,512]{1,0:T(8,128)(2,1)}), (bf16[512,512]{0,1:T(8,128)(2,1)}, bf16[512,512]{1,0:T(8,128)(2,1)})) %all-reduce.7.cloned.1.call-update) | async-done | bytes 1048592 | tf_op jit(solution)/shard_map/psum | solution.py:133
  242.7 1.2 convert_element_type.84
  244.0 0.4 fusion.16
  244.3 508.0 %all-reduce.5.cloned.1.call-done = (f32[512,64]{0,1:T(8,128)}, f32[512,64]{0,1:T(8,128)}, f32[512,64]{0,1:T(8,128)}, f32[64,512]{1,0:T(8,128)}) async-done(((f32[512,64]{0,1:T(8,128)}, f32[512,64]{0,1:T(8,128)}, f32[512,64]{0,1:T(8,128)}, f32[64,512]{1,0:T(8,128)}), (f32[512,64]{0,1:T(8,128)}, f32[512,64]{0,1:T(8,128)}, f32[512,64]{0,1:T(8,128)}, f32[64,512]{1,0:T(8,128)})) %all-reduce.5.cloned.1.call-update) | async-done | bytes 524304 | tf_op jit(solution)/shard_map/psum | solution.py:150
  752.3 1.6 broadcast_multiply_fusion.3
  753.9 0.7 broadcast_multiply_fusion
  754.6 1.5 fusion.55
  756.4 0.7 copy.44
  757.3 0.7 broadcast_multiply_fusion.1
  (77 shorter events, 3.4 us)
Async XLA Ops:
  7.2 63.1 %copy-start = (bf16[1,512,512]{2,1,0:T(8,128)(2,1)S(1)}, bf16[1,512,512]{2,1,0:T(8,128)(2,1)}, u32[]{:S(2)}) copy-start(bf16[1,512,512]{2,1,0:T(8,128)(2,1)} %param.17) | copy-start | bytes 1572868
  7.2 2.4 copy-start.1
  7.2 235.5 %all-reduce.7.cloned.1.call-start = ((), (), s32[]{:S(2)}) async-start(), calls=%async_computation.1 | async-start | bytes 2097152 | tf_op jit(solution)/shard_map/psum | solution.py:133
  11.4 59.9 %collective-permute-start = (bf16[1,2,128,128]{3,2,1,0:T(8,128)(2,1)S(1)}, bf16[1,2,128,128]{3,2,1,0:T(8,128)(2,1)S(1)}, u32[]{:S(2)}, u32[]{:S(2)}) collective-permute-start(bf16[1,2,128,128]{3,2,1,0:T(8,128)(2,1)S(1)} %bitcast_select_fusion.3), channel_id=1, source_target_pairs={{504,0},{0,8},{8,16},{16,24},{24,32},{32,40},{40,48},{48,56},{56,6... | collective-permute-start | bytes 196616 | tf_op jit(solution)/shard_map/ppermute | solution.py:17
  15.6 55.8 %collective-permute-start.1 = (bf16[1,2,128,128]{3,2,1,0:T(8,128)(2,1)S(1)}, bf16[1,2,128,128]{3,2,1,0:T(8,128)(2,1)S(1)}, u32[]{:S(2)}, u32[]{:S(2)}) collective-permute-start(bf16[1,2,128,128]{3,2,1,0:T(8,128)(2,1)S(1)} %bitcast_select_fusion.2), channel_id=1, source_target_pairs={{8,0},{16,8},{24,16},{32,24},{40,32},{48,40},{56,48},{64,56},{72,6... | collective-permute-start | bytes 196616 | tf_op jit(solution)/shard_map/ppermute | solution.py:17
  43.6 27.8 %collective-permute-start.2 = (bf16[1,2,128,128]{3,2,1,0:T(8,128)(2,1)S(1)}, bf16[1,2,128,128]{3,2,1,0:T(8,128)(2,1)S(1)}, u32[]{:S(2)}, u32[]{:S(2)}) collective-permute-start(bf16[1,2,128,128]{3,2,1,0:T(8,128)(2,1)S(1)} %bitcast_select_fusion.1), channel_id=1, source_target_pairs={{496,0},{504,8},{0,16},{8,24},{16,32},{24,40},{32,48},{40,56},{48,... | collective-permute-start | bytes 196616 | tf_op jit(solution)/shard_map/ppermute | solution.py:17
  46.1 23.7 %copy-start.8 = (bf16[512,64]{0,1:T(8,128)(2,1)S(1)}, bf16[512,64]{0,1:T(8,128)(2,1)}, u32[]{:S(2)}) copy-start(bf16[512,64]{0,1:T(8,128)(2,1)} %param.11) | copy-start | bytes 196612
  46.2 22.7 %copy-start.10 = (s32[1,4,2]{1,2,0:T(2,128)S(1)}, s32[1,4,2]{1,2,0:T(2,128)}, u32[]{:S(2)}) copy-start(s32[1,4,2]{1,2,0:T(2,128)} %param.15) | copy-start | bytes 100
  46.2 25.2 %collective-permute-start.3 = (bf16[1,2,128,128]{3,2,1,0:T(8,128)(2,1)S(1)}, bf16[1,2,128,128]{3,2,1,0:T(8,128)(2,1)S(1)}, u32[]{:S(2)}, u32[]{:S(2)}) collective-permute-start(bf16[1,2,128,128]{3,2,1,0:T(8,128)(2,1)S(1)} %bitcast_select_fusion), channel_id=1, source_target_pairs={{16,0},{24,8},{32,16},{40,24},{48,32},{56,40},{64,48},{72,56},{80,... | collective-permute-start | bytes 196616 | tf_op jit(solution)/shard_map/ppermute | solution.py:17
  68.9 0.7 copy-start.11
  70.2 0.8 copy-start.3
  83.3 1.7 copy-start.12
  91.0 31.5 %collective-permute-start.4 = (bf16[1,2,128,128]{3,1,2,0:T(2,128)(2,1)S(1)}, bf16[1,2,128,128]{3,1,2,0:T(2,128)(2,1)S(1)}, u32[]{:S(2)}, u32[]{:S(2)}) collective-permute-start(bf16[1,2,128,128]{3,1,2,0:T(2,128)(2,1)S(1)} %get-tuple-element.37), channel_id=1, source_target_pairs={{8,0},{16,8},{24,16},{32,24},{40,32},{48,40},{56,48},{64,56},{72,6... | collective-permute-start | bytes 196616 | tf_op jit(solution)/shard_map/ppermute | solution.py:17
  94.6 27.9 %collective-permute-start.7 = (bf16[1,2,128,128]{3,1,2,0:T(2,128)(2,1)S(1)}, bf16[1,2,128,128]{3,1,2,0:T(2,128)(2,1)S(1)}, u32[]{:S(2)}, u32[]{:S(2)}) collective-permute-start(bf16[1,2,128,128]{3,1,2,0:T(2,128)(2,1)S(1)} %get-tuple-element.38), channel_id=1, source_target_pairs={{496,0},{504,8},{0,16},{8,24},{16,32},{24,40},{32,48},{40,56},{48,... | collective-permute-start | bytes 196616 | tf_op jit(solution)/shard_map/ppermute | solution.py:17
  96.5 26.0 %collective-permute-start.6 = (bf16[1,2,128,128]{3,1,2,0:T(2,128)(2,1)S(1)}, bf16[1,2,128,128]{3,1,2,0:T(2,128)(2,1)S(1)}, u32[]{:S(2)}, u32[]{:S(2)}) collective-permute-start(bf16[1,2,128,128]{3,1,2,0:T(2,128)(2,1)S(1)} %get-tuple-element.39), channel_id=1, source_target_pairs={{16,0},{24,8},{32,16},{40,24},{48,32},{56,40},{64,48},{72,56},{80,... | collective-permute-start | bytes 196616 | tf_op jit(solution)/shard_map/ppermute | solution.py:17
  119.0 24.5 %collective-permute-start.5 = (bf16[1,2,128,128]{3,1,2,0:T(2,128)(2,1)S(1)}, bf16[1,2,128,128]{3,1,2,0:T(2,128)(2,1)S(1)}, u32[]{:S(2)}, u32[]{:S(2)}) collective-permute-start(bf16[1,2,128,128]{3,1,2,0:T(2,128)(2,1)S(1)} %get-tuple-element.40), channel_id=1, source_target_pairs={{504,0},{0,8},{8,16},{16,24},{24,32},{32,40},{40,48},{48,56},{56,6... | collective-permute-start | bytes 196616 | tf_op jit(solution)/shard_map/ppermute | solution.py:17
  144.0 0.8 copy-start.9
  144.9 0.8 copy-start.7
  146.9 605.5 %all-reduce.5.cloned.1.call-start = ((), (), s32[]{:S(2)}) async-start(), calls=%async_computation | async-start | bytes 1048576 | tf_op jit(solution)/shard_map/psum | solution.py:150
  242.7 1.2 copy-start.2
  752.3 1.6 copy-start.4
  756.1 1.1 copy-start.6
  756.4 0.9 copy-start.5
Sparse Core Ops, SparseCore 0:
  147.0 95.6 all-reduce.6
  247.0 505.2 all-reduce.4
where the time goes:
time: 766 us; the launch traced here: 765 us
  waiting for transfers between devices  622 us (81%)
  starting transfers between devices  85.7 us (11%)
  matrix products  21.9 us (3%)
  between operations  14.6 us (2%)
  local copies, waits for them, and re-layouts  12.5 us (2%)
  other arithmetic  8.39 us (1%)
    psum x1, waiting for transfers between devices, body(): lax.psum((grad_terms[0], grad_terms[1], grad_terms[2], grad_terms[3]), ('...  508 us
    psum x1, waiting for transfers between devices, body(): lax.psum(update_term.astype(jnp.bfloat16), 'tensor').astype(jnp.float32)  92.7 us
    ppermute x8, starting transfers between devices, shifted(): return lax.ppermute(block, axis, route)  85.6 us
    ppermute x8, waiting for transfers between devices, shifted(): return lax.ppermute(block, axis, route)  21.1 us
  transfers between devices with their start and end apart: 10, of which 3 were waited for; matrix products, arithmetic and copies ran while one was open for 1% of the time, Pallas kernels for 0%

commit v1 on v0

v1 whole, which is shorter than its diff:
```python
import functools
import math

import jax
import jax.numpy as jnp
from jax import lax
from jax.experimental import pallas as pl
from jax.experimental.pallas import tpu as pltpu
from jax.sharding import PartitionSpec as P

BLK = 128
HD = 64
D = 512
NBLK = 4
ROWS = NBLK * BLK
OFFSETS = (1, -1, 2, -2)
NY = 4
F32 = jnp.float32
BF16 = jnp.bfloat16
MESH = pl.DeviceIdType.MESH
EXP_SCALE = (1.0 / math.sqrt(HD)) / math.log(2.0)
SHRINK = 1.0 / math.sqrt(HD)


def nn(a, b):
    return lax.dot_general(a, b, (((1,), (0,)), ((), ())), preferred_element_type=F32)


def nt(a, b):
    return lax.dot_general(a, b, (((1,), (1,)), ((), ())), preferred_element_type=F32)


class Sizes:
    def __init__(self, dp, dom, t):
        self.DP, self.DOM, self.T = dp, dom, t
        nz = dom // NY
        self.ZR = min(4, nz)
        self.ZQ = nz // self.ZR
        self.NA = NY * self.ZR
        self.NB = self.ZQ * dp
        self.CR = 512 // self.NA
        self.BR = self.CR // self.NB
        self.SLAB = D // t
        self.factor = 1.0 / math.sqrt(dp * dom * ROWS)


def kernel(
    g,
    sb, nb, x_ref, wq_ref, wk_ref, wv_ref, wo_ref, cot_ref,
    upd_ref, br_ref, gq_ref, gk_ref, gv_ref, go_ref,
    unit, unit_t, x_t, wall, wo_t, wo_pad, inv_row, bm, kv_own, pool, pool_t, kvs,
    cg, mix_t, qg_t, xx, own, ret_s, ret_r,
    us, ur, ts, tr, rd_s, rd_r, gq_t,
    pay1, rsa1, tmp1, rsb_s1, rsb_r1, agb1, aga1,
    pay2, rsa2, tmp2, rsb_s2, rsb_r2, agb2, aga2,
    kv_ss, kv_rs, ret_ss, ret_rs, u_ss, u_rs, t_ss, t_rs, d_ss, d_rs,
    a1_ss, a1_rs, b1_ss, b1_rs, gb1_ss, gb1_rs, ga1_ss, ga1_rs,
    a2_ss, a2_rs, b2_ss, b2_rs, gb2_ss, gb2_rs, ga2_ss, ga2_rs,
):
    dp = lax.axis_index("dp")
    dom = lax.axis_index("dom")
    tn = lax.axis_index("tensor")
    y = lax.rem(dom, NY)
    z = dom // NY
    zr = lax.rem(z, g.ZR)
    zq = z // g.ZR
    my_a = y * g.ZR + zr
    my_b = dp * g.ZQ + zq

    def dom_peer(o):
        return (dp, lax.rem(dom + (o + g.DOM), g.DOM), tn)

    def t_index(k):
        return lax.rem(tn + k, g.T)

    def t_peer(k):
        return (dp, dom, t_index(k))

    a_offs = [(dy, dz) for dy in range(NY) for dz in range(g.ZR)][1:]
    b_offs = [(dd, dq) for dd in range(g.DP) for dq in range(g.ZQ)][1:]

    def a_peer(off):
        y2 = lax.rem(y + off[0], NY)
        r2 = lax.rem(zr + off[1], g.ZR)
        return y2 * g.ZR + r2, (dp, (zq * g.ZR + r2) * NY + y2, tn)

    def b_peer(off):
        d2 = lax.rem(dp + off[0], g.DP)
        q2 = lax.rem(zq + off[1], g.ZQ)
        return d2 * g.ZQ + q2, (d2, (q2 * g.ZR + zr) * NY + y, tn)

    peers = [dom_peer(o) for o in OFFSETS]
    peers += [t_peer(k) for k in range(1, g.T)]
    peers += [a_peer(off)[1] for off in a_offs]
    peers += [b_peer(off)[1] for off in b_offs]
    barrier = pltpu.get_barrier_semaphore()
    for peer in peers:
        pl.semaphore_signal(barrier, inc=1, device_id=peer, device_id_type=MESH)

    def remote(src, dst, ss, rs, peer):
        copy = pltpu.make_async_remote_copy(
            src_ref=src, dst_ref=dst, send_sem=ss, recv_sem=rs, device_id=peer, device_id_type=MESH
        )
        copy.start()
        return copy

    started = []

    wall[...] = jnp.concatenate(
        [wk_ref[...], wv_ref[...], wq_ref[...], jnp.zeros((D, HD), BF16)], axis=1
    )
    for b in range(NBLK):
        rows = slice(b * BLK, (b + 1) * BLK)
        xf = x_ref[rows, :].astype(F32)
        inv = lax.rsqrt(jnp.mean(xf * xf, axis=-1, keepdims=True) + 1e-05)
        unit[rows, :] = (xf * inv).astype(BF16)
    for b in range(NBLK):
        rows = slice(b * BLK, (b + 1) * BLK)
        block = nn(unit[rows, :], wall[:, : 2 * HD]).astype(BF16)
        kv_own[b] = block
        pool[b] = block
    for i in range(4):
        for c in range(2):
            kvs[i, c] = kv_own[sb[0, i, c]]
    pl.semaphore_wait(barrier, len(peers))
    kv_copies = []
    for i in (2, 3, 0, 1):
        kv_copies.append(
            remote(kvs.at[i], pool.at[pl.ds(NBLK + 2 * i, 2)], kv_ss.at[i], kv_rs.at[i], dom_peer(OFFSETS[i]))
        )

    wo_pad[0:HD, :] = jnp.zeros((HD, D), BF16)
    wo_pad[HD : 2 * HD, :] = wo_ref[...]
    for b in range(NBLK):
        rows = slice(b * BLK, (b + 1) * BLK)
        bm[b, 0:BLK, :] = nn(unit[rows, :], wall[:, 2 * HD :]).astype(BF16)
        bm[b, BLK : 2 * BLK, :] = nt(cot_ref[rows, :], wo_pad[...]).astype(BF16)
        pool_t[b] = kv_own[b].T
    for f in range(D // BLK):
        cols = slice(f * BLK, (f + 1) * BLK)
        for b in range(NBLK):
            x_t[cols, b * BLK : (b + 1) * BLK] = x_ref[b * BLK : (b + 1) * BLK, cols].T
        wo_t[cols, :] = wo_ref[:, cols].T
    square = jnp.zeros((1, ROWS), F32)
    for f in range(D // BLK):
        part = x_t[f * BLK : (f + 1) * BLK, :].astype(F32)
        square = square + jnp.sum(part * part, axis=0, keepdims=True)
    inv_lane = lax.rsqrt(square * (1.0 / D) + 1e-05)
    inv_row[...] = inv_lane
    for f in range(D // BLK):
        cols = slice(f * BLK, (f + 1) * BLK)
        unit_t[cols, :] = (x_t[cols, :].astype(F32) * inv_lane).astype(BF16)

    for copy in kv_copies:
        copy.wait_recv()
    for p in range(NBLK, 3 * NBLK):
        pool_t[p] = pool[p].T

    for b in range(NBLK):
        lists = [nb[b, n] for n in range(3)]
        kv_sel = jnp.concatenate([pool[b]] + [pool[i] for i in lists], axis=0)
        kv_sel_t = jnp.concatenate([pool_t[b]] + [pool_t[i] for i in lists], axis=1)
        both = nt(kv_sel, bm[b])
        scores = both[:, :BLK]
        prob_grad = both[:, BLK:]
        powers = jnp.exp2((scores - jnp.max(scores, axis=0, keepdims=True)) * EXP_SCALE)
        weights = powers * (1.0 / jnp.sum(powers, axis=0, keepdims=True))
        inner = jnp.sum(weights * prob_grad, axis=0, keepdims=True)
        score_low = (weights * (prob_grad - inner) * SHRINK).astype(BF16)
        pair = jnp.concatenate([score_low, weights.astype(BF16)], axis=1)
        grads = nn(pair, bm[b])
        for n in range(4):
            cg[4 * b + n] = grads[n * BLK : (n + 1) * BLK, :]
        outs = nn(kv_sel_t, pair)
        cols = slice(b * BLK, (b + 1) * BLK)
        qg_t[:, cols] = outs[0:HD, 0:BLK].astype(BF16)
        mix_t[:, cols] = outs[HD : 2 * HD, BLK : 2 * BLK].astype(BF16)

    def listed_sum(p, start):
        total = start
        for b in range(NBLK):
            for n in range(3):
                term = jnp.where(nb[b, n] == p, cg[4 * b + n + 1], 0.0)
                total = term if total is None else total + term
        return total

    ret_copies = []
    for i in (2, 3, 0, 1):
        for c in range(2):
            ret_s[i, c] = listed_sum(NBLK + 2 * i + c, None).astype(BF16)
        ret_copies.append(
            remote(ret_s.at[i], ret_r.at[i], ret_ss.at[i], ret_rs.at[i], dom_peer(-OFFSETS[i]))
        )

    for k in range(g.T):
        us[k] = nn(wo_t[k * g.SLAB : (k + 1) * g.SLAB, :], mix_t[...]).astype(BF16)
    u_copies = []
    for k in range(1, g.T):
        u_copies.append(
            remote(us.at[t_index(k)], ur.at[k - 1], u_ss.at[k - 1], u_rs.at[k - 1], t_peer(k))
        )

    def scatter_a(pay, rsa, ss, rs):
        copies = []
        for k, off in enumerate(a_offs):
            index, peer = a_peer(off)
            copies.append(remote(pay.at[index], rsa.at[k], ss.at[k], rs.at[k], peer))
        return copies

    def scatter_b(copies, pay, rsa, tmp, rsb_s, rsb_r, ss, rs):
        total = pay[my_a].astype(F32)
        for k, copy in enumerate(copies):
            copy.wait_recv()
            total = total + rsa[k].astype(F32)
        tmp[...] = total
        for j in range(g.NB):
            rsb_s[j] = tmp[j * g.BR : (j + 1) * g.BR, :]
        copies = []
        for k, off in enumerate(b_offs):
            index, peer = b_peer(off)
            copies.append(remote(rsb_s.at[index], rsb_r.at[k], ss.at[k], rs.at[k], peer))
        return copies

    def gather_b(copies, rsb_s, rsb_r, agb, ss, rs):
        total = rsb_s[my_b]
        for k, copy in enumerate(copies):
            copy.wait_recv()
            total = total + rsb_r[k]
        agb[my_b] = total
        copies = []
        for k, off in enumerate(b_offs):
            copies.append(remote(agb.at[my_b], agb.at[my_b], ss.at[k], rs.at[k], b_peer(off)[1]))
        return copies

    def gather_a(copies, agb, tmp, aga, ss, rs):
        for copy in copies:
            copy.wait_recv()
        for j in range(g.NB):
            tmp[j * g.BR : (j + 1) * g.BR, :] = agb[j]
        aga[my_a] = tmp[...].astype(BF16)
        copies = []
        for k, off in enumerate(a_offs):
            copies.append(remote(aga.at[my_a], aga.at[my_a], ss.at[k], rs.at[k], a_peer(off)[1]))
        return copies

    grad_q = nn(qg_t[...], unit[...])
    grad_o = nn(mix_t[...], cot_ref[...])
    lane_blocks = D // BLK
    for a in range(g.NA):
        r, c = a // lane_blocks, a % lane_blocks
        row = r * g.CR
        cols = slice(c * BLK, (c + 1) * BLK)
        if row < HD:
            pay1[a] = grad_q[row : row + g.CR, cols].astype(BF16)
        else:
            pay1[a] = grad_o[row - HD : row - HD + g.CR, cols].astype(BF16)
    a1 = scatter_a(pay1, rsa1, a1_ss, a1_rs)
    started += a1

    for j in range(NBLK):
        own[j] = listed_sum(j, cg[4 * j])
    for b in range(NBLK):
        rows = slice(b * BLK, (b + 1) * BLK)
        query_grad = qg_t[:, rows].astype(F32).T.astype(BF16)
        xx[rows, 2 * HD :] = jnp.concatenate([query_grad, jnp.zeros((BLK, HD), BF16)], axis=1)

    b1 = scatter_b(a1, pay1, rsa1, tmp1, rsb_s1, rsb_r1, b1_ss, b1_rs)
    started += b1

    for copy in ret_copies:
        copy.wait_recv()
    for j in range(NBLK):
        total = own[j]
        for i in range(4):
            for c in range(2):
                total = total + jnp.where(sb[0, i, c] == j, ret_r[i, c].astype(F32), 0.0)
        xx[j * BLK : (j + 1) * BLK, : 2 * HD] = total.astype(BF16)

    for a in range(g.NA):
        rows = slice(a * g.CR, (a + 1) * g.CR)
        pay2[a] = nn(unit_t[rows, :], xx[:, : 2 * HD]).astype(BF16)
    a2 = scatter_a(pay2, rsa2, a2_ss, a2_rs)
    started += a2

    for k in range(g.T):
        rows = slice(k * g.SLAB, (k + 1) * g.SLAB)
        ts[k] = nt(wall[rows, :], xx[...]).astype(BF16)
    t_copies = []
    for k in range(1, g.T):
        t_copies.append(
            remote(ts.at[t_index(k)], tr.at[k - 1], t_ss.at[k - 1], t_rs.at[k - 1], t_peer(k))
        )
    dots = jnp.zeros((1, ROWS), F32)
    for k in range(g.T):
        rows = slice(k * g.SLAB, (k + 1) * g.SLAB)
        dots = dots + jnp.sum(ts[k].astype(F32) * x_t[rows, :].astype(F32), axis=0, keepdims=True)
    rd_s[...] = dots
    d_copies = []
    for k in range(1, g.T):
        d_copies.append(remote(rd_s, rd_r.at[k - 1], d_ss.at[k - 1], d_rs.at[k - 1], t_peer(k)))

    gb1 = gather_b(b1, rsb_s1, rsb_r1, agb1, gb1_ss, gb1_rs)
    b2 = scatter_b(a2, pay2, rsa2, tmp2, rsb_s2, rsb_r2, b2_ss, b2_rs)
    ga1 = gather_a(gb1, agb1, tmp1, aga1, ga1_ss, ga1_rs)

    total = us[tn].astype(F32)
    for k, copy in enumerate(u_copies):
        copy.wait_recv()
        total = total + ur[k].astype(F32)
    upd_ref[0] = total.T.astype(BF16)

    gb2 = gather_b(b2, rsb_s2, rsb_r2, agb2, gb2_ss, gb2_rs)

    total = ts[tn].astype(F32)
    for k, copy in enumerate(t_copies):
        copy.wait_recv()
        total = total + tr[k].astype(F32)
    for k, copy in enumerate(d_copies):
        copy.wait_recv()
        dots = dots + rd_r[k]
    inv_lane = inv_row[...]
    slab = x_t[pl.ds(pl.multiple_of(tn * g.SLAB, g.SLAB), g.SLAB), :].astype(F32) * inv_lane
    row_mean = dots * inv_lane * (1.0 / D)
    br_ref[0] = (inv_lane * (total - slab * row_mean)).T.astype(BF16)

    ga2 = gather_a(gb2, agb2, tmp2, aga2, ga2_ss, ga2_rs)

    for copy in ga1:
        copy.wait_recv()
    for a in range(g.NA):
        r, c = a // lane_blocks, a % lane_blocks
        row = r * g.CR
        cols = slice(c * BLK, (c + 1) * BLK)
        chunk = aga1[a].astype(F32) * g.factor
        if row < HD:
            gq_t[row : row + g.CR, cols] = chunk
        else:
            go_ref[row - HD : row - HD + g.CR, cols] = chunk
    for c in range(lane_blocks):
        cols = slice(c * BLK, (c + 1) * BLK)
        gq_ref[cols, :] = gq_t[:, cols].T
    for copy in ga2:
        copy.wait_recv()
    for a in range(g.NA):
        rows = slice(a * g.CR, (a + 1) * g.CR)
        chunk = aga2[a].astype(F32) * g.factor
        gk_ref[rows, :] = chunk[:, :HD]
        gv_ref[rows, :] = chunk[:, HD:]

    started += kv_copies + ret_copies + u_copies + t_copies + d_copies
    started += gb1 + b2 + ga1 + gb2 + ga2
    for copy in started:
        copy.wait_send()


def body(g, states, w_query, w_key, w_value, w_out, send_blocks, neighbor_blocks, cotangent):
    vmem = pl.BlockSpec(memory_space=pltpu.VMEM)
    smem = pl.BlockSpec(memory_space=pltpu.SMEM)
    sem = pltpu.SemaphoreType.DMA
    blocks = (BLK, 2 * HD)
    reduce_bufs = [
        pltpu.VMEM((g.NA, g.CR, 128), BF16),
        pltpu.VMEM((max(g.NA - 1, 1), g.CR, 128), BF16),
        pltpu.VMEM((g.CR, 128), F32),
        pltpu.VMEM((g.NB, g.BR, 128), F32),
        pltpu.VMEM((max(g.NB - 1, 1), g.BR, 128), F32),
        pltpu.VMEM((g.NB, g.BR, 128), F32),
        pltpu.VMEM((g.NA, g.CR, 128), BF16),
    ]
    na, nbb, nt_ = max(g.NA - 1, 1), max(g.NB - 1, 1), max(g.T - 1, 1)
    reduce_sems = [sem((n,)) for n in (na, na, nbb, nbb, nbb, nbb, na, na)]
    out = pl.pallas_call(
        functools.partial(kernel, g),
        out_shape=[
            jax.ShapeDtypeStruct((1, ROWS, g.SLAB), BF16),
            jax.ShapeDtypeStruct((1, ROWS, g.SLAB), BF16),
            jax.ShapeDtypeStruct((D, HD), F32),
            jax.ShapeDtypeStruct((D, HD), F32),
            jax.ShapeDtypeStruct((D, HD), F32),
            jax.ShapeDtypeStruct((HD, D), F32),
        ],
        in_specs=[smem, smem] + [vmem] * 6,
        out_specs=[vmem] * 6,
        scratch_shapes=[
            pltpu.VMEM((ROWS, D), BF16),
            pltpu.VMEM((D, ROWS), BF16),
            pltpu.VMEM((D, ROWS), BF16),
            pltpu.VMEM((D, 4 * HD), BF16),
            pltpu.VMEM((D, HD), BF16),
            pltpu.VMEM((2 * HD, D), BF16),
            pltpu.VMEM((1, ROWS), F32),
            pltpu.VMEM((NBLK, 2 * BLK, 2 * HD), BF16),
            pltpu.VMEM((NBLK,) + blocks, BF16),
            pltpu.VMEM((3 * NBLK,) + blocks, BF16),
            pltpu.VMEM((3 * NBLK,) + blocks, BF16),
            pltpu.VMEM((4, 2) + blocks, BF16),
            pltpu.VMEM((4 * NBLK,) + blocks, F32),
            pltpu.VMEM((HD, ROWS), BF16),
            pltpu.VMEM((HD, ROWS), BF16),
            pltpu.VMEM((ROWS, 4 * HD), BF16),
            pltpu.VMEM((NBLK,) + blocks, F32),
            pltpu.VMEM((4, 2) + blocks, BF16),
            pltpu.VMEM((4, 2) + blocks, BF16),
            pltpu.VMEM((g.T, g.SLAB, ROWS), BF16),
            pltpu.VMEM((nt_, g.SLAB, ROWS), BF16),
            pltpu.VMEM((g.T, g.SLAB, ROWS), BF16),
            pltpu.VMEM((nt_, g.SLAB, ROWS), BF16),
            pltpu.VMEM((1, ROWS), F32),
            pltpu.VMEM((nt_, 1, ROWS), F32),
            pltpu.VMEM((HD, D), F32),
        ]
        + reduce_bufs
        + reduce_bufs
        + [sem((4,))] * 4
        + [sem((nt_,))] * 6
        + reduce_sems
        + reduce_sems,
        compiler_params=pltpu.CompilerParams(
            collective_id=0, has_side_effects=True, vmem_limit_bytes=40 * 1024 * 1024
        ),
        name="layer",
    )(
        send_blocks, neighbor_blocks, states[0], w_query, w_key, w_value, w_out, cotangent[0]
    )
    return tuple(out)


def solution(mesh):
    placed = (
        P("dp", "dom", None),
        P(None, "tensor"),
        P(None, "tensor"),
        P(None, "tensor"),
        P("tensor", None),
        P("dom", None, None),
        P("dom", None),
        P("dp", "dom", None),
    )
    g = Sizes(mesh.shape["dp"], mesh.shape["dom"], mesh.shape["tensor"])
    return jax.shard_map(
        functools.partial(body, g),
        mesh=mesh,
        in_specs=placed,
        out_specs=(
            P("dp", "dom", "tensor"),
            P("dp", "dom", "tensor"),
            P(None, "tensor"),
            P(None, "tensor"),
            P(None, "tensor"),
            P("tensor", None),
        ),
        check_vma=False,
    )
```

time: 766 us -> 108 us (0.14)
  waiting for transfers between devices: 622 us -> 0 us
  Pallas kernels: 0 us -> 97.6 us
  starting transfers between devices: 85.7 us -> 0 us
  matrix products: 21.9 us -> 0 us
  between operations: 14.6 us -> 0.72 us
  other arithmetic: 8.39 us -> 0 us
    psum x2 -> x0, waiting for transfers between devices: 601 us -> none  [the longest x1 508 us: body(): lax.psum((grad_terms[0], grad_terms[1], grad_terms[2], grad_terms[3]), ('...]
    pallas_call x0 -> x1, Pallas kernels: none -> 97.6 us  [body(): pl.pallas_call(functools.partial(kernel, g), out_shape=[jax.ShapeDtypeStr...]
    ppermute x8 -> x0, starting transfers between devices: 85.6 us -> none  [shifted(): return lax.ppermute(block, axis, route)]
    ppermute x8 -> x0, waiting for transfers between devices: 21.1 us -> none  [shifted(): return lax.ppermute(block, axis, route)]
    dot_general x18 -> x0, matrix products: 20.4 us -> none  [the longest x5 10.5 us: product(): return jnp.einsum(form, left, right, preferred_element_type=jnp.float32)]
  transfers between devices with their start and end apart: 10 -> 0, of which waited for: 3 -> 0; matrix products, arithmetic and copies ran while one was open for 1% -> 0% of each run, Pallas kernels for 0% -> 0%
where the time goes in v1:
time: 108 us
  Pallas kernels  97.6 us (90%)
  local copies, waits for them, and re-layouts  9.2 us (9%)
    pallas_call x1, Pallas kernels, body(): pl.pallas_call(functools.partial(kernel, g), out_shape=[jax.ShapeDtypeStr...  97.6 us
    unnamed x13, local copies, waits for them, and re-layouts  5.43 us
    pallas_call x5, local copies, waits for them, and re-layouts, body(): pl.pallas_call(functools.partial(kernel, g), out_shape=[jax.ShapeDtypeStr...  3.77 us

profile of v1, /device:TPU:6, one launch (start us, length us, event | category | flops | bytes accessed | tf_op | source)
XLA Modules:
  0.0 107.6 jit_solution(4851858379249640122)
XLA Ops:
  0.6 0.0 copy-start
  0.6 0.8 copy.14.sb
  1.5 1.0 copy.15.wq_ref
  2.4 1.0 copy.16.wk_ref
  3.4 0.0 copy-start.2
  3.4 0.0 copy-start.3
  3.4 1.0 copy.17.wv_ref
  4.4 0.0 copy-done
  4.4 0.0 copy-done.2
  4.4 0.0 copy-done.3
  4.4 0.0 copy-start.1
  4.5 1.0 copy-done.1
  5.5 97.6 %layer.1 = (bf16[1,512,64]{2,1,0:T(8,128)(2,1)S(1)}, bf16[1,512,64]{2,1,0:T(8,128)(2,1)S(1)}, f32[512,64]{1,0:T(8,128)S(1)}, f32[512,64]{1,0:T(8,128)S(1)}, f32[...) custom-call(s32[1,4,2]{2,1,0:T(4,128)S(1)} %copy.14.sb, s32[4,3]{1,0:T(4,128)S(1)} %copy-done.3, bf16[512,512]{1,0:T(8,128)(2,1)S(1)} %bitcast.2, ...), custom_call_target="tpu_custom_call" | custom-call | tf_op jit(solution)/shard_map/layer/pallas_call | solution.py:372
  103.1 0.7 copy.18
  103.9 0.7 copy.19
  104.6 0.8 copy.20
  105.4 0.8 copy.21
  106.1 0.8 copy.22
  106.9 0.7 copy.24
Async XLA Ops:
  0.6 3.8 %copy-start = (bf16[1,512,512]{2,1,0:T(8,128)(2,1)S(1)}, bf16[1,512,512]{2,1,0:T(8,128)(2,1)}, u32[]{:S(2)}) copy-start(bf16[1,512,512]{2,1,0:T(8,128)(2,1)} %param.8) | copy-start | bytes 1572868
  3.4 1.0 copy-start.2
  3.4 1.0 copy-start.3
  4.4 1.0 copy-start.1

commit v2 on v1

--- a/solution.py
+++ b/solution.py
@@ -39,23 +39,21 @@
         self.NA = NY * self.ZR
         self.NB = self.ZQ * dp
         self.CR = 512 // self.NA
-        self.BR = self.CR // self.NB
         self.SLAB = D // t
         self.factor = 1.0 / math.sqrt(dp * dom * ROWS)
 
 
 def kernel(
     g,
-    sb, nb, x_ref, wq_ref, wk_ref, wv_ref, wo_ref, cot_ref,
-    upd_ref, br_ref, gq_ref, gk_ref, gv_ref, go_ref,
-    unit, unit_t, x_t, wall, wo_t, wo_pad, inv_row, bm, kv_own, pool, pool_t, kvs,
+    sb, nb, x_any, wq_any, wk_any, wv_any, wo_any, cot_any,
+    upd_ref, br_ref, w_ref,
+    x_ref, cot_ref, in_sems, unit, x_t, wall_t, wall, wo_t, wo_pad, inv_row, bm, kv_own, pool, pool_t, kvs,
     cg, mix_t, qg_t, xx, own, ret_s, ret_r,
-    us, ur, ts, tr, rd_s, rd_r, gq_t,
-    pay1, rsa1, tmp1, rsb_s1, rsb_r1, agb1, aga1,
-    pay2, rsa2, tmp2, rsb_s2, rsb_r2, agb2, aga2,
+    us, ur, ts, tr, rd_s, rd_r, kvg_t,
+    pay1, rsa1, bb1, aga1, pay2, rsa2, bb2, aga2,
     kv_ss, kv_rs, ret_ss, ret_rs, u_ss, u_rs, t_ss, t_rs, d_ss, d_rs,
-    a1_ss, a1_rs, b1_ss, b1_rs, gb1_ss, gb1_rs, ga1_ss, ga1_rs,
-    a2_ss, a2_rs, b2_ss, b2_rs, gb2_ss, gb2_rs, ga2_ss, ga2_rs,
+    a1_ss, a1_rs, b1_ss, b1_rs, ga1_ss, ga1_rs,
+    a2_ss, a2_rs, b2_ss, b2_rs, ga2_ss, ga2_rs,
 ):
     dp = lax.axis_index("dp")
     dom = lax.axis_index("dom")
@@ -93,6 +91,21 @@
     peers += [t_peer(k) for k in range(1, g.T)]
     peers += [a_peer(off)[1] for off in a_offs]
     peers += [b_peer(off)[1] for off in b_offs]
+    fetches = [
+        pltpu.make_async_copy(src, dst, in_sems.at[i])
+        for i, (src, dst) in enumerate(
+            (
+                (x_any, x_ref),
+                (wk_any, wall_t.at[0:HD]),
+                (wv_any, wall_t.at[HD : 2 * HD]),
+                (wq_any, wall_t.at[2 * HD : 3 * HD]),
+                (wo_any, wo_pad.at[HD : 2 * HD]),
+                (cot_any, cot_ref),
+            )
+        )
+    ]
+    for copy in fetches:
+        copy.start()
     barrier = pltpu.get_barrier_semaphore()
     for peer in peers:
         pl.semaphore_signal(barrier, inc=1, device_id=peer, device_id_type=MESH)
@@ -106,9 +119,9 @@
 
     started = []
 
-    wall[...] = jnp.concatenate(
-        [wk_ref[...], wv_ref[...], wq_ref[...], jnp.zeros((D, HD), BF16)], axis=1
-    )
+    fetches[0].wait()
+    fetches[1].wait()
+    fetches[2].wait()
     for b in range(NBLK):
         rows = slice(b * BLK, (b + 1) * BLK)
         xf = x_ref[rows, :].astype(F32)
@@ -116,12 +129,12 @@
         unit[rows, :] = (xf * inv).astype(BF16)
     for b in range(NBLK):
         rows = slice(b * BLK, (b + 1) * BLK)
-        block = nn(unit[rows, :], wall[:, : 2 * HD]).astype(BF16)
+        block = nt(unit[rows, :], wall_t[: 2 * HD, :]).astype(BF16)
         kv_own[b] = block
         pool[b] = block
     for i in range(4):
         for c in range(2):
-            kvs[i, c] = kv_own[sb[0, i, c]]
+            kvs[i, c] = kv_own[sb[0, c, i]]
     pl.semaphore_wait(barrier, len(peers))
     kv_copies = []
     for i in (2, 3, 0, 1):
@@ -130,26 +143,27 @@
         )
 
     wo_pad[0:HD, :] = jnp.zeros((HD, D), BF16)
-    wo_pad[HD : 2 * HD, :] = wo_ref[...]
+    wall_t[3 * HD :, :] = jnp.zeros((HD, D), BF16)
+    fetches[3].wait()
+    fetches[4].wait()
+    fetches[5].wait()
     for b in range(NBLK):
         rows = slice(b * BLK, (b + 1) * BLK)
-        bm[b, 0:BLK, :] = nn(unit[rows, :], wall[:, 2 * HD :]).astype(BF16)
+        bm[b, 0:BLK, :] = nt(unit[rows, :], wall_t[2 * HD :, :]).astype(BF16)
         bm[b, BLK : 2 * BLK, :] = nt(cot_ref[rows, :], wo_pad[...]).astype(BF16)
         pool_t[b] = kv_own[b].T
     for f in range(D // BLK):
         cols = slice(f * BLK, (f + 1) * BLK)
         for b in range(NBLK):
             x_t[cols, b * BLK : (b + 1) * BLK] = x_ref[b * BLK : (b + 1) * BLK, cols].T
-        wo_t[cols, :] = wo_ref[:, cols].T
+        wo_t[cols, :] = wo_pad[HD : 2 * HD, cols].T
+        wall[cols, :] = wall_t[:, cols].T
     square = jnp.zeros((1, ROWS), F32)
     for f in range(D // BLK):
         part = x_t[f * BLK : (f + 1) * BLK, :].astype(F32)
         square = square + jnp.sum(part * part, axis=0, keepdims=True)
     inv_lane = lax.rsqrt(square * (1.0 / D) + 1e-05)
     inv_row[...] = inv_lane
-    for f in range(D // BLK):
-        cols = slice(f * BLK, (f + 1) * BLK)
-        unit_t[cols, :] = (x_t[cols, :].astype(F32) * inv_lane).astype(BF16)
 
     for copy in kv_copies:
         copy.wait_recv()
@@ -207,37 +221,24 @@
             copies.append(remote(pay.at[index], rsa.at[k], ss.at[k], rs.at[k], peer))
         return copies
 
-    def scatter_b(copies, pay, rsa, tmp, rsb_s, rsb_r, ss, rs):
+    def spread_b(copies, pay, rsa, bb, ss, rs):
         total = pay[my_a].astype(F32)
         for k, copy in enumerate(copies):
             copy.wait_recv()
             total = total + rsa[k].astype(F32)
-        tmp[...] = total
-        for j in range(g.NB):
-            rsb_s[j] = tmp[j * g.BR : (j + 1) * g.BR, :]
+        bb[my_b] = total.astype(BF16)
         copies = []
         for k, off in enumerate(b_offs):
-            index, peer = b_peer(off)
-            copies.append(remote(rsb_s.at[index], rsb_r.at[k], ss.at[k], rs.at[k], peer))
+            copies.append(remote(bb.at[my_b], bb.at[my_b], ss.at[k], rs.at[k], b_peer(off)[1]))
         return copies
 
-    def gather_b(copies, rsb_s, rsb_r, agb, ss, rs):
-        total = rsb_s[my_b]
-        for k, copy in enumerate(copies):
-            copy.wait_recv()
-            total = total + rsb_r[k]
-        agb[my_b] = total
-        copies = []
-        for k, off in enumerate(b_offs):
-            copies.append(remote(agb.at[my_b], agb.at[my_b], ss.at[k], rs.at[k], b_peer(off)[1]))
-        return copies
-
-    def gather_a(copies, agb, tmp, aga, ss, rs):
+    def gather_a(copies, bb, aga, ss, rs):
         for copy in copies:
             copy.wait_recv()
-        for j in range(g.NB):
-            tmp[j * g.BR : (j + 1) * g.BR, :] = agb[j]
-        aga[my_a] = tmp[...].astype(BF16)
+        total = bb[0].astype(F32)
+        for j in range(1, g.NB):
+            total = total + bb[j].astype(F32)
+        aga[my_a] = total.astype(BF16)
         copies = []
         for k, off in enumerate(a_offs):
             copies.append(remote(aga.at[my_a], aga.at[my_a], ss.at[k], rs.at[k], a_peer(off)[1]))
@@ -264,7 +265,7 @@
         query_grad = qg_t[:, rows].astype(F32).T.astype(BF16)
         xx[rows, 2 * HD :] = jnp.concatenate([query_grad, jnp.zeros((BLK, HD), BF16)], axis=1)
 
-    b1 = scatter_b(a1, pay1, rsa1, tmp1, rsb_s1, rsb_r1, b1_ss, b1_rs)
+    b1 = spread_b(a1, pay1, rsa1, bb1, b1_ss, b1_rs)
     started += b1
 
     for copy in ret_copies:
@@ -273,12 +274,15 @@
         total = own[j]
         for i in range(4):
             for c in range(2):
-                total = total + jnp.where(sb[0, i, c] == j, ret_r[i, c].astype(F32), 0.0)
-        xx[j * BLK : (j + 1) * BLK, : 2 * HD] = total.astype(BF16)
-
+                total = total + jnp.where(sb[0, c, i] == j, ret_r[i, c].astype(F32), 0.0)
+        total = total.astype(BF16)
+        xx[j * BLK : (j + 1) * BLK, : 2 * HD] = total
+        kvg_t[:, j * BLK : (j + 1) * BLK] = total.T
+
+    grad_kv = nn(kvg_t[...], unit[...])
     for a in range(g.NA):
-        rows = slice(a * g.CR, (a + 1) * g.CR)
-        pay2[a] = nn(unit_t[rows, :], xx[:, : 2 * HD]).astype(BF16)
+        r, c = a // lane_blocks, a % lane_blocks
+        pay2[a] = grad_kv[r * g.CR : (r + 1) * g.CR, c * BLK : (c + 1) * BLK].astype(BF16)
     a2 = scatter_a(pay2, rsa2, a2_ss, a2_rs)
     started += a2
 
@@ -299,17 +303,14 @@
     for k in range(1, g.T):
         d_copies.append(remote(rd_s, rd_r.at[k - 1], d_ss.at[k - 1], d_rs.at[k - 1], t_peer(k)))
 
-    gb1 = gather_b(b1, rsb_s1, rsb_r1, agb1, gb1_ss, gb1_rs)
-    b2 = scatter_b(a2, pay2, rsa2, tmp2, rsb_s2, rsb_r2, b2_ss, b2_rs)
-    ga1 = gather_a(gb1, agb1, tmp1, aga1, ga1_ss, ga1_rs)
+    b2 = spread_b(a2, pay2, rsa2, bb2, b2_ss, b2_rs)
+    ga1 = gather_a(b1, bb1, aga1, ga1_ss, ga1_rs)
 
     total = us[tn].astype(F32)
     for k, copy in enumerate(u_copies):
         copy.wait_recv()
         total = total + ur[k].astype(F32)
-    upd_ref[0] = total.T.astype(BF16)
-
-    gb2 = gather_b(b2, rsb_s2, rsb_r2, agb2, gb2_ss, gb2_rs)
+    upd_ref[...] = total.astype(BF16)
 
     total = ts[tn].astype(F32)
     for k, copy in enumerate(t_copies):
@@ -321,36 +322,51 @@
     inv_lane = inv_row[...]
     slab = x_t[pl.ds(pl.multiple_of(tn * g.SLAB, g.SLAB), g.SLAB), :].astype(F32) * inv_lane
     row_mean = dots * inv_lane * (1.0 / D)
-    br_ref[0] = (inv_lane * (total - slab * row_mean)).T.astype(BF16)
-
-    ga2 = gather_a(gb2, agb2, tmp2, aga2, ga2_ss, ga2_rs)
+    br_ref[...] = (inv_lane * (total - slab * row_mean)).astype(BF16)
+
+    ga2 = gather_a(b2, bb2, aga2, ga2_ss, ga2_rs)
 
     for copy in ga1:
         copy.wait_recv()
     for a in range(g.NA):
         r, c = a // lane_blocks, a % lane_blocks
-        row = r * g.CR
-        cols = slice(c * BLK, (c + 1) * BLK)
-        chunk = aga1[a].astype(F32) * g.factor
-        if row < HD:
-            gq_t[row : row + g.CR, cols] = chunk
-        else:
-            go_ref[row - HD : row - HD + g.CR, cols] = chunk
-    for c in range(lane_blocks):
-        cols = slice(c * BLK, (c + 1) * BLK)
-        gq_ref[cols, :] = gq_t[:, cols].T
+        w_ref[0, r * g.CR : (r + 1) * g.CR, c * BLK : (c + 1) * BLK] = aga1[a].astype(F32) * g.factor
     for copy in ga2:
         copy.wait_recv()
     for a in range(g.NA):
-        rows = slice(a * g.CR, (a + 1) * g.CR)
-        chunk = aga2[a].astype(F32) * g.factor
-        gk_ref[rows, :] = chunk[:, :HD]
-        gv_ref[rows, :] = chunk[:, HD:]
+        r, c = a // lane_blocks, a % lane_blocks
+        w_ref[1, r * g.CR : (r + 1) * g.CR, c * BLK : (c + 1) * BLK] = aga2[a].astype(F32) * g.factor
 
     started += kv_copies + ret_copies + u_copies + t_copies + d_copies
-    started += gb1 + b2 + ga1 + gb2 + ga2
+    started += b2 + ga1 + ga2
     for copy in started:
         copy.wait_send()
+
+
+def write_kernel(upd, br, w, o0, o1, o2, o3, o4, o5, sems):
+    pairs = [
+        (upd, o0), (br, o1),
+        (w.at[0, 0:HD], o2), (w.at[1, 0:HD], o3), (w.at[1, HD : 2 * HD], o4), (w.at[0, HD : 2 * HD], o5),
+    ]
+    copies = [pltpu.make_async_copy(src, dst, sems.at[i]) for i, (src, dst) in enumerate(pairs)]
+    for copy in copies:
+        copy.start()
+    for copy in copies:
+        copy.wait()
+
+
+def write_out(g, upd, br, w):
+    slab = jax.ShapeDtypeStruct((g.SLAB, ROWS), BF16)
+    grad = jax.ShapeDtypeStruct((HD, D), F32)
+    return pl.pallas_call(
+        write_kernel,
+        out_shape=[slab, slab, grad, grad, grad, grad],
+        in_specs=[pl.BlockSpec(memory_space=pl.ANY)] * 3,
+        out_specs=[pl.BlockSpec(memory_space=pltpu.HBM)] * 6,
+        scratch_shapes=[pltpu.SemaphoreType.DMA((6,))],
+        compiler_params=pltpu.CompilerParams(vmem_limit_bytes=4 * 1024 * 1024),
+        name="write",
+    )(upd, br, w)
 
 
 def body(g, states, w_query, w_key, w_value, w_out, send_blocks, neighbor_blocks, cotangent):
@@ -361,30 +377,27 @@
     reduce_bufs = [
         pltpu.VMEM((g.NA, g.CR, 128), BF16),
         pltpu.VMEM((max(g.NA - 1, 1), g.CR, 128), BF16),
-        pltpu.VMEM((g.CR, 128), F32),
-        pltpu.VMEM((g.NB, g.BR, 128), F32),
-        pltpu.VMEM((max(g.NB - 1, 1), g.BR, 128), F32),
-        pltpu.VMEM((g.NB, g.BR, 128), F32),
+        pltpu.VMEM((g.NB, g.CR, 128), BF16),
         pltpu.VMEM((g.NA, g.CR, 128), BF16),
     ]
     na, nbb, nt_ = max(g.NA - 1, 1), max(g.NB - 1, 1), max(g.T - 1, 1)
-    reduce_sems = [sem((n,)) for n in (na, na, nbb, nbb, nbb, nbb, na, na)]
+    reduce_sems = [sem((n,)) for n in (na, na, nbb, nbb, na, na)]
     out = pl.pallas_call(
         functools.partial(kernel, g),
         out_shape=[
-            jax.ShapeDtypeStruct((1, ROWS, g.SLAB), BF16),
-            jax.ShapeDtypeStruct((1, ROWS, g.SLAB), BF16),
-            jax.ShapeDtypeStruct((D, HD), F32),
-            jax.ShapeDtypeStruct((D, HD), F32),
-            jax.ShapeDtypeStruct((D, HD), F32),
-            jax.ShapeDtypeStruct((HD, D), F32),
+            jax.ShapeDtypeStruct((g.SLAB, ROWS), BF16),
+            jax.ShapeDtypeStruct((g.SLAB, ROWS), BF16),
+            jax.ShapeDtypeStruct((2, 2 * HD, D), F32),
         ],
-        in_specs=[smem, smem] + [vmem] * 6,
-        out_specs=[vmem] * 6,
+        in_specs=[smem, smem] + [pl.BlockSpec(memory_space=pltpu.HBM)] * 6,
+        out_specs=[vmem] * 3,
         scratch_shapes=[
             pltpu.VMEM((ROWS, D), BF16),
+            pltpu.VMEM((ROWS, D), BF16),
+            sem((6,)),
+            pltpu.VMEM((ROWS, D), BF16),
             pltpu.VMEM((D, ROWS), BF16),
-            pltpu.VMEM((D, ROWS), BF16),
+            pltpu.VMEM((4 * HD, D), BF16),
             pltpu.VMEM((D, 4 * HD), BF16),
             pltpu.VMEM((D, HD), BF16),
             pltpu.VMEM((2 * HD, D), BF16),
@@ -407,7 +420,7 @@
             pltpu.VMEM((nt_, g.SLAB, ROWS), BF16),
             pltpu.VMEM((1, ROWS), F32),
             pltpu.VMEM((nt_, 1, ROWS), F32),
-            pltpu.VMEM((HD, D), F32),
+            pltpu.VMEM((2 * HD, ROWS), BF16),
         ]
         + reduce_bufs
         + reduce_bufs
@@ -420,9 +433,10 @@
         ),
         name="layer",
     )(
-        send_blocks, neighbor_blocks, states[0], w_query, w_key, w_value, w_out, cotangent[0]
+        jnp.swapaxes(send_blocks, 1, 2), neighbor_blocks, states[0], w_query.T, w_key.T, w_value.T, w_out, cotangent[0]
     )
-    return tuple(out)
+    done = write_out(g, *out)
+    return (done[0].T[None], done[1].T[None], done[2].T, done[3].T, done[4].T, done[5])
 
 
 def solution(mesh):

time: 108 us -> 96.8 us (0.90)
  Pallas kernels: 97.6 us -> 89.5 us
  local copies, waits for them, and re-layouts: 9.2 us -> 6.12 us
    pallas_call x1, Pallas kernels: 97.6 us -> 88.6 us  [body(): pl.pallas_call(functools.partial(kernel, g), out_shape=[jax.ShapeDtypeStr...]
    pallas_call x5 -> x0, local copies, waits for them, and re-layouts: 3.77 us -> none  [body(): pl.pallas_call(functools.partial(kernel, g), out_shape=[jax.ShapeDtypeStr...]
    unnamed x13 -> x16, local copies, waits for them, and re-layouts: 5.43 us -> 6.12 us
where the time goes in v2:
time: 96.8 us; the launch traced here: 96.3 us
  Pallas kernels  89.5 us (92%)
  local copies, waits for them, and re-layouts  6.12 us (6%)
    pallas_call x1, Pallas kernels, body(): pl.pallas_call(functools.partial(kernel, g), out_shape=[jax.ShapeDtypeStr...  88.6 us
    unnamed x16, local copies, waits for them, and re-layouts  6.12 us

profile of v2, /device:TPU:6, one launch (start us, length us, event | category | flops | bytes accessed | tf_op | source)
XLA Modules:
  0.0 96.3 jit_solution(14437425682429720780)
XLA Ops:
  0.6 0.0 copy-start.6
  0.6 0.0 copy-start.7
  0.7 0.7 copy-done.6
  1.3 0.0 copy-done.7
  1.3 0.0 copy-start
  1.3 1.0 %copy-done = bf16[1,512,512]{2,1,0:T(8,128)(2,1)S(1)} copy-done((bf16[1,512,512]{2,1,0:T(8,128)(2,1)S(1)}, bf16[1,512,512]{2,1,0:T(8,128)(2,1)}, u32[]{:S(2)}) %copy-start) | copy-done | bytes 524312
  2.4 0.0 copy-start.1
  2.4 1.0 %copy-done.1 = bf16[1,512,512]{2,1,0:T(8,128)(2,1)S(1)} copy-done((bf16[1,512,512]{2,1,0:T(8,128)(2,1)S(1)}, bf16[1,512,512]{2,1,0:T(8,128)(2,1)}, u32[]{:S(2)}) %copy-start.1) | copy-done | bytes 524312
  3.4 0.0 copy-start.2
  3.4 0.8 copy-done.2
  4.3 0.0 copy-start.3
  4.3 0.8 copy-done.3
  5.1 0.0 copy-start.4
  5.1 0.8 copy-done.4
  5.9 0.0 copy-start.5
  5.9 0.8 copy-done.5
  6.8 88.6 %layer.1 = (bf16[64,512]{1,0:T(8,128)(2,1)S(1)}, bf16[64,512]{1,0:T(8,128)(2,1)S(1)}, f32[2,128,512]{2,1,0:T(8,128)S(1)}) custom-call(s32[1,2,4]{2,1,0:T(2,128)S(1)} %bitcast.20, s32[4,3]{1,0:T(4,128)S(1)} %copy-done.6, bf16[512,512]{1,0:T(8,128)(2,1)S(1)} %bitcast.15, bf16[64,512]{1,0:T(8,128)(2,1)S(1)} %bitcast.17, bf16[64,512]{1,0:T(8,128)(2,1)S(1)} %bitcast.18, ...), custom_call_target="tpu_custom_call" | custom-call | tf_op jit(solution)/shard_map/layer/pallas_call | solution.py:385
  95.4 0.9 write.1
Async XLA Ops:
  0.6 0.7 copy-start.6
  0.6 0.7 copy-start.7
  1.3 1.0 %copy-start = (bf16[1,512,512]{2,1,0:T(8,128)(2,1)S(1)}, bf16[1,512,512]{2,1,0:T(8,128)(2,1)}, u32[]{:S(2)}) copy-start(bf16[1,512,512]{2,1,0:T(8,128)(2,1)} %param.8) | copy-start | bytes 1572868
  2.4 1.0 %copy-start.1 = (bf16[1,512,512]{2,1,0:T(8,128)(2,1)S(1)}, bf16[1,512,512]{2,1,0:T(8,128)(2,1)}, u32[]{:S(2)}) copy-start(bf16[1,512,512]{2,1,0:T(8,128)(2,1)} %param.15) | copy-start | bytes 1572868
  3.4 0.8 copy-start.2
  4.3 0.8 copy-start.3
  5.1 0.8 copy-start.4
  5.9 0.8 copy-start.5

commit v3 on v2

--- a/solution.py
+++ b/solution.py
@@ -45,13 +45,13 @@
 
 def kernel(
     g,
-    sb, nb, x_any, wq_any, wk_any, wv_any, wo_any, cot_any,
+    sb_any, nb_any, x_any, wq_any, wk_any, wv_any, wo_any, cot_any,
     upd_ref, br_ref, w_ref,
-    x_ref, cot_ref, in_sems, unit, x_t, wall_t, wall, wo_t, wo_pad, inv_row, bm, kv_own, pool, pool_t, kvs,
+    sb, nb, x_ref, cot_ref, in_sems, unit_b, x_t, wall_t, wall, wo_t, wo_pad, inv_row, bm, kv_own, pool, pool_t, kvs,
     cg, mix_t, qg_t, xx, own, ret_s, ret_r,
-    us, ur, ts, tr, rd_s, rd_r, kvg_t,
+    us, ur, ts, tr, rd_s, rd_r, kvg_t, rows_s, rows_r, gkv,
     pay1, rsa1, bb1, aga1, pay2, rsa2, bb2, aga2,
-    kv_ss, kv_rs, ret_ss, ret_rs, u_ss, u_rs, t_ss, t_rs, d_ss, d_rs,
+    kv_ss, kv_rs, ret_ss, ret_rs, row_ss, row_rs, u_ss, u_rs, t_ss, t_rs, d_ss, d_rs,
     a1_ss, a1_rs, b1_ss, b1_rs, ga1_ss, ga1_rs,
     a2_ss, a2_rs, b2_ss, b2_rs, ga2_ss, ga2_rs,
 ):
@@ -87,6 +87,11 @@
         q2 = lax.rem(zq + off[1], g.ZQ)
         return d2 * g.ZQ + q2, (d2, (q2 * g.ZR + zr) * NY + y, tn)
 
+    def far(size, d):
+        return min(d, size - d)
+
+    b_offs.sort(key=lambda off: -(16 * off[0] + 4 * off[1] if not off[0] else 16 - 4 * off[1]))
+    a_offs.sort(key=lambda off: -(far(NY, off[0]) + (3 if off[1] else 0)))
     peers = [dom_peer(o) for o in OFFSETS]
     peers += [t_peer(k) for k in range(1, g.T)]
     peers += [a_peer(off)[1] for off in a_offs]
@@ -101,6 +106,8 @@
                 (wq_any, wall_t.at[2 * HD : 3 * HD]),
                 (wo_any, wo_pad.at[HD : 2 * HD]),
                 (cot_any, cot_ref),
+                (sb_any, sb),
+                (nb_any, nb),
             )
         )
     ]
@@ -126,12 +133,14 @@
         rows = slice(b * BLK, (b + 1) * BLK)
         xf = x_ref[rows, :].astype(F32)
         inv = lax.rsqrt(jnp.mean(xf * xf, axis=-1, keepdims=True) + 1e-05)
-        unit[rows, :] = (xf * inv).astype(BF16)
+        unit_b[b] = (xf * inv).astype(BF16)
     for b in range(NBLK):
         rows = slice(b * BLK, (b + 1) * BLK)
-        block = nt(unit[rows, :], wall_t[: 2 * HD, :]).astype(BF16)
+        block = nt(unit_b[b], wall_t[: 2 * HD, :]).astype(BF16)
         kv_own[b] = block
         pool[b] = block
+    fetches[6].wait()
+    fetches[7].wait()
     for i in range(4):
         for c in range(2):
             kvs[i, c] = kv_own[sb[0, c, i]]
@@ -142,6 +151,27 @@
             remote(kvs.at[i], pool.at[pl.ds(NBLK + 2 * i, 2)], kv_ss.at[i], kv_rs.at[i], dom_peer(OFFSETS[i]))
         )
 
+    def send_wraps(i):
+        there = dom + OFFSETS[i]
+        return jnp.logical_or(there < 0, there >= g.DOM)
+
+    def recv_wraps(i):
+        there = dom - OFFSETS[i]
+        return jnp.logical_or(there < 0, there >= g.DOM)
+
+    def row_copy(i):
+        return pltpu.make_async_remote_copy(
+            src_ref=rows_s.at[i], dst_ref=rows_r.at[i], send_sem=row_ss.at[i], recv_sem=row_rs.at[i],
+            device_id=dom_peer(OFFSETS[i]), device_id_type=MESH,
+        )
+
+    for i in (2, 3, 0, 1):
+        @pl.when(send_wraps(i))
+        def _(i=i):
+            for c in range(2):
+                rows_s[i, c] = unit_b[sb[0, c, i]]
+            row_copy(i).start()
+
     wo_pad[0:HD, :] = jnp.zeros((HD, D), BF16)
     wall_t[3 * HD :, :] = jnp.zeros((HD, D), BF16)
     fetches[3].wait()
@@ -149,7 +179,7 @@
     fetches[5].wait()
     for b in range(NBLK):
         rows = slice(b * BLK, (b + 1) * BLK)
-        bm[b, 0:BLK, :] = nt(unit[rows, :], wall_t[2 * HD :, :]).astype(BF16)
+        bm[b, 0:BLK, :] = nt(unit_b[b], wall_t[2 * HD :, :]).astype(BF16)
         bm[b, BLK : 2 * BLK, :] = nt(cot_ref[rows, :], wo_pad[...]).astype(BF16)
         pool_t[b] = kv_own[b].T
     for f in range(D // BLK):
@@ -244,7 +274,8 @@
             copies.append(remote(aga.at[my_a], aga.at[my_a], ss.at[k], rs.at[k], a_peer(off)[1]))
         return copies
 
-    grad_q = nn(qg_t[...], unit[...])
+    unit = unit_b[...].reshape(ROWS, D)
+    grad_q = nn(qg_t[...], unit)
     grad_o = nn(mix_t[...], cot_ref[...])
     lane_blocks = D // BLK
     for a in range(g.NA):
@@ -268,23 +299,39 @@
     b1 = spread_b(a1, pay1, rsa1, bb1, b1_ss, b1_rs)
     started += b1
 
-    for copy in ret_copies:
-        copy.wait_recv()
+    def returned(i, c, j):
+        return jnp.where(sb[0, c, i] == j, ret_r[i, c].astype(F32), 0.0)
+
+    for i, copy in zip((2, 3, 0, 1), ret_copies):
+        @pl.when(jnp.logical_not(send_wraps(i)))
+        def _(i=i, copy=copy):
+            copy.wait_recv()
+            for j in range(NBLK):
+                own[j] = own[j] + (returned(i, 0, j) + returned(i, 1, j))
     for j in range(NBLK):
-        total = own[j]
-        for i in range(4):
+        kvg_t[:, j * BLK : (j + 1) * BLK] = own[j].astype(BF16).T
+    gkv[...] = nn(kvg_t[...], unit)
+    for i in (2, 3, 0, 1):
+        @pl.when(recv_wraps(i))
+        def _(i=i):
+            row_copy(i).wait_recv()
             for c in range(2):
-                total = total + jnp.where(sb[0, c, i] == j, ret_r[i, c].astype(F32), 0.0)
-        total = total.astype(BF16)
-        xx[j * BLK : (j + 1) * BLK, : 2 * HD] = total
-        kvg_t[:, j * BLK : (j + 1) * BLK] = total.T
-
-    grad_kv = nn(kvg_t[...], unit[...])
+                gkv[...] += nn(ret_s[i, c].T, rows_r[i, c])
     for a in range(g.NA):
         r, c = a // lane_blocks, a % lane_blocks
-        pay2[a] = grad_kv[r * g.CR : (r + 1) * g.CR, c * BLK : (c + 1) * BLK].astype(BF16)
+        pay2[a] = gkv[r * g.CR : (r + 1) * g.CR, c * BLK : (c + 1) * BLK].astype(BF16)
     a2 = scatter_a(pay2, rsa2, a2_ss, a2_rs)
     started += a2
+    b2 = spread_b(a2, pay2, rsa2, bb2, b2_ss, b2_rs)
+
+    for i, copy in zip((2, 3, 0, 1), ret_copies):
+        @pl.when(send_wraps(i))
+        def _(i=i, copy=copy):
+            copy.wait_recv()
+            for j in range(NBLK):
+                own[j] = own[j] + (returned(i, 0, j) + returned(i, 1, j))
+    for j in range(NBLK):
+        xx[j * BLK : (j + 1) * BLK, : 2 * HD] = own[j].astype(BF16)
 
     for k in range(g.T):
         rows = slice(k * g.SLAB, (k + 1) * g.SLAB)
@@ -303,7 +350,6 @@
     for k in range(1, g.T):
         d_copies.append(remote(rd_s, rd_r.at[k - 1], d_ss.at[k - 1], d_rs.at[k - 1], t_peer(k)))
 
-    b2 = spread_b(a2, pay2, rsa2, bb2, b2_ss, b2_rs)
     ga1 = gather_a(b1, bb1, aga1, ga1_ss, ga1_rs)
 
     total = us[tn].astype(F32)
@@ -341,6 +387,10 @@
     started += b2 + ga1 + ga2
     for copy in started:
         copy.wait_send()
+    for i in range(4):
+        @pl.when(send_wraps(i))
+        def _(i=i):
+            row_copy(i).wait_send()
 
 
 def write_kernel(upd, br, w, o0, o1, o2, o3, o4, o5, sems):
@@ -371,7 +421,6 @@
 
 def body(g, states, w_query, w_key, w_value, w_out, send_blocks, neighbor_blocks, cotangent):
     vmem = pl.BlockSpec(memory_space=pltpu.VMEM)
-    smem = pl.BlockSpec(memory_space=pltpu.SMEM)
     sem = pltpu.SemaphoreType.DMA
     blocks = (BLK, 2 * HD)
     reduce_bufs = [
@@ -382,6 +431,10 @@
     ]
     na, nbb, nt_ = max(g.NA - 1, 1), max(g.NB - 1, 1), max(g.T - 1, 1)
     reduce_sems = [sem((n,)) for n in (na, na, nbb, nbb, na, na)]
+    inputs = (
+        jnp.swapaxes(send_blocks, 1, 2), neighbor_blocks, states[0],
+        w_query.T, w_key.T, w_value.T, w_out, cotangent[0],
+    )
     out = pl.pallas_call(
         functools.partial(kernel, g),
         out_shape=[
@@ -389,13 +442,15 @@
             jax.ShapeDtypeStruct((g.SLAB, ROWS), BF16),
             jax.ShapeDtypeStruct((2, 2 * HD, D), F32),
         ],
-        in_specs=[smem, smem] + [pl.BlockSpec(memory_space=pltpu.HBM)] * 6,
+        in_specs=[pl.BlockSpec(memory_space=pltpu.HBM)] * 8,
         out_specs=[vmem] * 3,
         scratch_shapes=[
+            pltpu.SMEM((1, 2, 4), jnp.int32),
+            pltpu.SMEM((NBLK, 3), jnp.int32),
             pltpu.VMEM((ROWS, D), BF16),
             pltpu.VMEM((ROWS, D), BF16),
-            sem((6,)),
-            pltpu.VMEM((ROWS, D), BF16),
+            sem((8,)),
+            pltpu.VMEM((NBLK, BLK, D), BF16),
             pltpu.VMEM((D, ROWS), BF16),
             pltpu.VMEM((4 * HD, D), BF16),
             pltpu.VMEM((D, 4 * HD), BF16),
@@ -421,10 +476,13 @@
             pltpu.VMEM((1, ROWS), F32),
             pltpu.VMEM((nt_, 1, ROWS), F32),
             pltpu.VMEM((2 * HD, ROWS), BF16),
+            pltpu.VMEM((4, 2, BLK, D), BF16),
+            pltpu.VMEM((4, 2, BLK, D), BF16),
+            pltpu.VMEM((2 * HD, D), F32),
         ]
         + reduce_bufs
         + reduce_bufs
-        + [sem((4,))] * 4
+        + [sem((4,))] * 6
         + [sem((nt_,))] * 6
         + reduce_sems
         + reduce_sems,
@@ -433,7 +491,7 @@
         ),
         name="layer",
     )(
-        jnp.swapaxes(send_blocks, 1, 2), neighbor_blocks, states[0], w_query.T, w_key.T, w_value.T, w_out, cotangent[0]
+        *[pltpu.with_memory_space_constraint(value, pltpu.HBM) for value in inputs]
     )
     done = write_out(g, *out)
     return (done[0].T[None], done[1].T[None], done[2].T, done[3].T, done[4].T, done[5])

time: 96.8 us -> 92.4 us (0.955)
  the two profiles are of different devices: /device:TPU:6 before, /device:TPU:1 now
where the time goes in v3:
time: 92.4 us; the launch traced here: 92.2 us
  Pallas kernels  91.5 us (99%)
    pallas_call x1, Pallas kernels, body(): pl.pallas_call(functools.partial(kernel, g), out_shape=[jax.ShapeDtypeStr...  90.7 us

profile of v3, /device:TPU:1, one launch (start us, length us, event | category | flops | bytes accessed | tf_op | source)
XLA Modules:
  0.0 92.2 jit_solution(11290478382140883172)
XLA Ops:
  0.6 90.7 %layer.1 = (bf16[64,512]{1,0:T(8,128)(2,1)S(1)}, bf16[64,512]{1,0:T(8,128)(2,1)S(1)}, f32[2,128,512]{2,1,0:T(8,128)S(1)}) custom-call(s32[1,2,4]{2,1,0:T(2,128)} %bitcast.20, s32[4,3]{1,0:T(4,128)} %nb_any.1, bf16[512,512]{1,0:T(8,128)(2,1)} %bitcast.15, bf16[64,512]{1,0:T(8,128)(2,1)} %bitcast.17, bf16[64,512]{1,0:T(8,128)(2,1)} %bitcast.18, ...), custom_call_target="tpu_custom_call" | custom-call | tf_op jit(solution)/shard_map/layer/pallas_call | solution.py:438
  91.3 0.9 write.1

commit v4 on v3

--- a/solution.py
+++ b/solution.py
@@ -51,7 +51,7 @@
     cg, mix_t, qg_t, xx, own, ret_s, ret_r,
     us, ur, ts, tr, rd_s, rd_r, kvg_t, rows_s, rows_r, gkv,
     pay1, rsa1, bb1, aga1, pay2, rsa2, bb2, aga2,
-    kv_ss, kv_rs, ret_ss, ret_rs, row_ss, row_rs, u_ss, u_rs, t_ss, t_rs, d_ss, d_rs,
+    kv_ss, kv_rs, ret_ss, ret_rs, row_ss, row_rs, pass_ss, pass_rs, u_ss, u_rs, t_ss, t_rs, d_ss, d_rs,
     a1_ss, a1_rs, b1_ss, b1_rs, ga1_ss, ga1_rs,
     a2_ss, a2_rs, b2_ss, b2_rs, ga2_ss, ga2_rs,
 ):
@@ -151,6 +151,8 @@
             remote(kvs.at[i], pool.at[pl.ds(NBLK + 2 * i, 2)], kv_ss.at[i], kv_rs.at[i], dom_peer(OFFSETS[i]))
         )
 
+    half = lax.rem(tn, 2)
+
     def send_wraps(i):
         there = dom + OFFSETS[i]
         return jnp.logical_or(there < 0, there >= g.DOM)
@@ -161,15 +163,20 @@
 
     def row_copy(i):
         return pltpu.make_async_remote_copy(
-            src_ref=rows_s.at[i], dst_ref=rows_r.at[i], send_sem=row_ss.at[i], recv_sem=row_rs.at[i],
+            src_ref=rows_s.at[i], dst_ref=rows_r.at[i, half], send_sem=row_ss.at[i], recv_sem=row_rs.at[i],
             device_id=dom_peer(OFFSETS[i]), device_id_type=MESH,
+        )
+
+    def pass_copy(i):
+        return pltpu.make_async_remote_copy(
+            src_ref=rows_r.at[i, half], dst_ref=rows_r.at[i, half], send_sem=pass_ss.at[i], recv_sem=pass_rs.at[i],
+            device_id=(dp, dom, tn + 1 - 2 * half), device_id_type=MESH,
         )
 
     for i in (2, 3, 0, 1):
         @pl.when(send_wraps(i))
         def _(i=i):
-            for c in range(2):
-                rows_s[i, c] = unit_b[sb[0, c, i]]
+            rows_s[i] = unit_b[sb[0, half, i]]
             row_copy(i).start()
 
     wo_pad[0:HD, :] = jnp.zeros((HD, D), BF16)
@@ -296,8 +303,12 @@
         query_grad = qg_t[:, rows].astype(F32).T.astype(BF16)
         xx[rows, 2 * HD :] = jnp.concatenate([query_grad, jnp.zeros((BLK, HD), BF16)], axis=1)
 
-    b1 = spread_b(a1, pay1, rsa1, bb1, b1_ss, b1_rs)
-    started += b1
+
+    for i in (2, 3, 0, 1):
+        @pl.when(recv_wraps(i))
+        def _(i=i):
+            row_copy(i).wait_recv()
+            pass_copy(i).start()
 
     def returned(i, c, j):
         return jnp.where(sb[0, c, i] == j, ret_r[i, c].astype(F32), 0.0)
@@ -314,7 +325,7 @@
     for i in (2, 3, 0, 1):
         @pl.when(recv_wraps(i))
         def _(i=i):
-            row_copy(i).wait_recv()
+            pass_copy(i).wait_recv()
             for c in range(2):
                 gkv[...] += nn(ret_s[i, c].T, rows_r[i, c])
     for a in range(g.NA):
@@ -322,6 +333,8 @@
         pay2[a] = gkv[r * g.CR : (r + 1) * g.CR, c * BLK : (c + 1) * BLK].astype(BF16)
     a2 = scatter_a(pay2, rsa2, a2_ss, a2_rs)
     started += a2
+    b1 = spread_b(a1, pay1, rsa1, bb1, b1_ss, b1_rs)
+    started += b1
     b2 = spread_b(a2, pay2, rsa2, bb2, b2_ss, b2_rs)
 
     for i, copy in zip((2, 3, 0, 1), ret_copies):
@@ -391,6 +404,10 @@
         @pl.when(send_wraps(i))
         def _(i=i):
             row_copy(i).wait_send()
+
+        @pl.when(recv_wraps(i))
+        def _(i=i):
+            pass_copy(i).wait_send()
 
 
 def write_kernel(upd, br, w, o0, o1, o2, o3, o4, o5, sems):
@@ -476,13 +493,13 @@
             pltpu.VMEM((1, ROWS), F32),
             pltpu.VMEM((nt_, 1, ROWS), F32),
             pltpu.VMEM((2 * HD, ROWS), BF16),
-            pltpu.VMEM((4, 2, BLK, D), BF16),
+            pltpu.VMEM((4, BLK, D), BF16),
             pltpu.VMEM((4, 2, BLK, D), BF16),
             pltpu.VMEM((2 * HD, D), F32),
         ]
         + reduce_bufs
         + reduce_bufs
-        + [sem((4,))] * 6
+        + [sem((4,))] * 8
         + [sem((nt_,))] * 6
         + reduce_sems
         + reduce_sems,

time: 92.4 us -> 84 us (0.909)
  the two profiles are of different devices: /device:TPU:1 before, /device:TPU:6 now
where the time goes in v4:
time: 84 us; the launch traced here: 83.8 us
  Pallas kernels  83.2 us (99%)
    pallas_call x1, Pallas kernels, body(): pl.pallas_call(functools.partial(kernel, g), out_shape=[jax.ShapeDtypeStr...  82.3 us

profile of v4, /device:TPU:6, one launch (start us, length us, event | category | flops | bytes accessed | tf_op | source)
XLA Modules:
  0.0 83.8 jit_solution(13299697277546764118)
XLA Ops:
  0.6 82.3 %layer.1 = (bf16[64,512]{1,0:T(8,128)(2,1)S(1)}, bf16[64,512]{1,0:T(8,128)(2,1)S(1)}, f32[2,128,512]{2,1,0:T(8,128)S(1)}) custom-call(s32[1,2,4]{2,1,0:T(2,128)} %bitcast.20, s32[4,3]{1,0:T(4,128)} %nb_any.1, bf16[512,512]{1,0:T(8,128)(2,1)} %bitcast.15, bf16[64,512]{1,0:T(8,128)(2,1)} %bitcast.17, bf16[64,512]{1,0:T(8,128)(2,1)} %bitcast.18, ...), custom_call_target="tpu_custom_call" | custom-call | tf_op jit(solution)/shard_map/layer/pallas_call | solution.py:455
  82.9 0.9 %write.1 = (bf16[64,512]{1,0:T(8,128)(2,1)}, bf16[64,512]{1,0:T(8,128)(2,1)}, f32[64,512]{1,0:T(8,128)}, f32[64,512]{1,0:T(8,128)}, f32[64,512]{1,0:T(8,128)}, /*index=5*/f32[64,512]{1,0:T(8,128)}) custom-call(bf16[64,512]{1,0:T(8,128)(2,1)S(1)} %get-tuple-element.15.upd, bf16[64,512]{1,0:T(8,128)(2,1)S(1)} %get-tuple-element.16.br, ...), custom_call_target="tpu_custom_call" | custom-call | tf_op jit(solution)/shard_map/write/pallas_call | solution.py:428

commit v5 on v4

--- a/solution.py
+++ b/solution.py
@@ -96,6 +96,10 @@
     peers += [t_peer(k) for k in range(1, g.T)]
     peers += [a_peer(off)[1] for off in a_offs]
     peers += [b_peer(off)[1] for off in b_offs]
+    barrier = pltpu.get_barrier_semaphore()
+    for peer in peers:
+        pl.semaphore_signal(barrier, inc=1, device_id=peer, device_id_type=MESH)
+
     fetches = [
         pltpu.make_async_copy(src, dst, in_sems.at[i])
         for i, (src, dst) in enumerate(
@@ -113,10 +117,6 @@
     ]
     for copy in fetches:
         copy.start()
-    barrier = pltpu.get_barrier_semaphore()
-    for peer in peers:
-        pl.semaphore_signal(barrier, inc=1, device_id=peer, device_id_type=MESH)
-
     def remote(src, dst, ss, rs, peer):
         copy = pltpu.make_async_remote_copy(
             src_ref=src, dst_ref=dst, send_sem=ss, recv_sem=rs, device_id=peer, device_id_type=MESH
@@ -153,13 +153,14 @@
 
     half = lax.rem(tn, 2)
 
+    def late(part):
+        return jnp.logical_or(part < 2, part >= g.DOM - 2)
+
     def send_wraps(i):
-        there = dom + OFFSETS[i]
-        return jnp.logical_or(there < 0, there >= g.DOM)
+        return late(lax.rem(dom + (OFFSETS[i] + g.DOM), g.DOM))
 
     def recv_wraps(i):
-        there = dom - OFFSETS[i]
-        return jnp.logical_or(there < 0, there >= g.DOM)
+        return late(dom)
 
     def row_copy(i):
         return pltpu.make_async_remote_copy(
@@ -333,9 +334,9 @@
         pay2[a] = gkv[r * g.CR : (r + 1) * g.CR, c * BLK : (c + 1) * BLK].astype(BF16)
     a2 = scatter_a(pay2, rsa2, a2_ss, a2_rs)
     started += a2
+    b2 = spread_b(a2, pay2, rsa2, bb2, b2_ss, b2_rs)
     b1 = spread_b(a1, pay1, rsa1, bb1, b1_ss, b1_rs)
     started += b1
-    b2 = spread_b(a2, pay2, rsa2, bb2, b2_ss, b2_rs)
 
     for i, copy in zip((2, 3, 0, 1), ret_copies):
         @pl.when(send_wraps(i))
@@ -363,6 +364,8 @@
     for k in range(1, g.T):
         d_copies.append(remote(rd_s, rd_r.at[k - 1], d_ss.at[k - 1], d_rs.at[k - 1], t_peer(k)))
 
+
+    ga2 = gather_a(b2, bb2, aga2, ga2_ss, ga2_rs)
     ga1 = gather_a(b1, bb1, aga1, ga1_ss, ga1_rs)
 
     total = us[tn].astype(F32)
@@ -383,7 +386,6 @@
     row_mean = dots * inv_lane * (1.0 / D)
     br_ref[...] = (inv_lane * (total - slab * row_mean)).astype(BF16)
 
-    ga2 = gather_a(b2, bb2, aga2, ga2_ss, ga2_rs)
 
     for copy in ga1:
         copy.wait_recv()

time: 84 us -> 83.5 us (level)
  no operation moved by 1% of the time
where the time goes in v5:
time: 83.5 us; the launch traced here: 83.3 us
  Pallas kernels  82.7 us (99%)
    pallas_call x1, Pallas kernels, body(): pl.pallas_call(functools.partial(kernel, g), out_shape=[jax.ShapeDtypeStr...  81.8 us

profile of v5, /device:TPU:6, one launch (start us, length us, event | category | flops | bytes accessed | tf_op | source)
XLA Modules:
  0.0 83.3 jit_solution(14237576752645776828)
XLA Ops:
  0.6 81.8 %layer.1 = (bf16[64,512]{1,0:T(8,128)(2,1)S(1)}, bf16[64,512]{1,0:T(8,128)(2,1)S(1)}, f32[2,128,512]{2,1,0:T(8,128)S(1)}) custom-call(s32[1,2,4]{2,1,0:T(2,128)} %bitcast.20, s32[4,3]{1,0:T(4,128)} %nb_any.1, bf16[512,512]{1,0:T(8,128)(2,1)} %bitcast.15, bf16[64,512]{1,0:T(8,128)(2,1)} %bitcast.17, bf16[64,512]{1,0:T(8,128)(2,1)} %bitcast.18, ...), custom_call_target="tpu_custom_call" | custom-call | tf_op jit(solution)/shard_map/layer/pallas_call | solution.py:457
  82.4 0.9 %write.1 = (bf16[64,512]{1,0:T(8,128)(2,1)}, bf16[64,512]{1,0:T(8,128)(2,1)}, f32[64,512]{1,0:T(8,128)}, f32[64,512]{1,0:T(8,128)}, f32[64,512]{1,0:T(8,128)}, /*index=5*/f32[64,512]{1,0:T(8,128)}) custom-call(bf16[64,512]{1,0:T(8,128)(2,1)S(1)} %get-tuple-element.15.upd, bf16[64,512]{1,0:T(8,128)(2,1)S(1)} %get-tuple-element.16.br, ...), custom_call_target="tpu_custom_call" | custom-call | tf_op jit(solution)/shard_map/write/pallas_call | solution.py:430
